TPU v7x, 256 devices: a whole 4x4x8 slice. The times are simulated.
256 devices in a mesh: section: 8 (over y, core), chan: 32 (over z, x).
Axes of the slice: x: 4, y: 4, z: 8, core: 2. Of those that a mesh axis runs over, the one named last changes fastest.
Arguments:
- prompt: bfloat16 [192, 8192], P(None, 'chan'), may hold values from -6 to 6
- norm_gain: bfloat16 [8, 8192], P('section', 'chan'), may hold values from 0.5 to 1.5
- in_weight: bfloat16 [8, 8192, 3, 8192], P('section', None, None, 'chan'), may hold values from -0.0625 to 0.0625
- feat_taps: float32 [8, 3, 3, 8192], P('section', None, None, 'chan'), may hold values from -3 to 3
- fir_taps: float32 [8, 128, 512], P('section', None, 'chan'), may hold values from -0.5 to 0.5
- residues: float32 [8, 16, 512], P('section', None, 'chan'), may hold values from -0.2 to 0.2
- decay: float32 [8, 16, 512], P('section', None, 'chan'), may hold values from 0.002 to 0.1
Outputs:
- section_out: bfloat16 [8, 192, 8192], P('section', None, 'chan')
All inputs are finite; a program needn't handle non-finite values.
Results may differ from a plain program's by a relative error of at most 0.019.
Values may be sent and summed in bfloat16 or wider, within the bound.
A program may use at most 128 MiB of HBM per device.

v0:
```python
import jax
import jax.numpy as jnp
from jax import lax
from jax.sharding import PartitionSpec as P

BLOCK_TOK = 64
NBLOCKS = 3
EPSILON = 1e-06


def shifted(value, axis, steps):
    count = lax.axis_size(axis)
    initial, last = (max(0, -steps), min(count, count - steps))
    return lax.ppermute(value, axis, [(source, source + steps) for source in range(initial, last)])


def body(prompt, norm_gain, in_weight, feat_taps, fir_taps, residues, decay):
    block_len = BLOCK_TOK
    num_blocks = NBLOCKS
    width = in_weight.shape[1]
    local = prompt.shape[1]
    groups_local = fir_taps.shape[2]
    group_size = local // groups_local
    fir_len = fir_taps.shape[1]
    sections = lax.axis_size("section")
    section_idx = lax.axis_index("section")
    is_medium = section_idx % 2 == 0
    weight = in_weight[0].reshape(width, 3 * local)
    tap_rows = feat_taps[0]
    fir_section = fir_taps[0]
    residue_section = residues[0]
    rate_section = decay[0]
    out_pos = jnp.arange(block_len)
    in_pos = jnp.arange(fir_len + block_len)
    fir_lag = out_pos[:, None] + fir_len - in_pos[None, :]
    fir_ok = (fir_lag >= 0) & (fir_lag < fir_len)
    fir_table = jnp.where(fir_ok[None], fir_section.T[:, jnp.clip(fir_lag, 0, fir_len - 1)], 0.0)
    inner_lag = out_pos[:, None] - (in_pos[None, :] - fir_len)
    inner_ok = (inner_lag >= 0) & (in_pos[None, :] >= fir_len)
    lag_values = out_pos.astype(jnp.float32)
    powers = jnp.exp(-rate_section[None, :, :] * lag_values[:, None, None])
    modal = jnp.einsum("ng,jng->jg", residue_section, powers, precision=lax.Precision.HIGHEST)
    modal_table = jnp.where(inner_ok[None], modal.T[:, jnp.clip(inner_lag, 0, block_len - 1)], 0.0)
    toeplitz = jnp.where(is_medium, fir_table, modal_table)
    carry_coef = residue_section[None] * jnp.exp(
        -rate_section[None] * (lag_values + 1.0)[:, None, None]
    )
    carry_coef = jnp.where(is_medium, 0.0, carry_coef)
    feed_coef = jnp.exp(-rate_section[None] * (block_len - 1.0 - lag_values)[:, None, None])
    block_decay = jnp.exp(-rate_section * block_len)

    def add_rows(shard_piece):
        return jnp.dot(shard_piece, weight, preferred_element_type=jnp.float32)

    def turn(carried, turn_index):
        incoming, proj_cache, kv_cache, modal_state, out_buffer = carried
        which = turn_index - section_idx
        is_live = (which >= 0) & (which < num_blocks)
        begin_row = jnp.clip(which, 0, num_blocks - 1) * block_len
        first_rows = lax.dynamic_slice_in_dim(prompt, begin_row, block_len, 0)
        rows_in = jnp.where(section_idx == 0, first_rows, incoming)
        inputs_f = rows_in.astype(jnp.float32)
        partial_sq = jnp.sum(inputs_f * inputs_f, axis=1)
        squares = lax.psum(partial_sq, "chan")
        normed = (
            inputs_f * lax.rsqrt(squares[:, None] / width + EPSILON) * norm_gain.astype(jnp.float32)
        ).astype(jnp.bfloat16)
        projected = add_rows(lax.all_gather(normed, "chan", axis=1, tiled=True))
        projected = projected.reshape(block_len, 3, local)
        extended = jnp.concatenate([proj_cache, projected], axis=0)
        features = (
            tap_rows[0] * extended[2:] + tap_rows[1] * extended[1:-1] + tap_rows[2] * extended[:-2]
        )
        product_kv = features[:, 1] * features[:, 2]
        window = jnp.concatenate([kv_cache, product_kv], axis=0)
        grouped = window.reshape(fir_len + block_len, groups_local, group_size)
        convolved = jnp.einsum("gts,sgk->tgk", toeplitz, grouped, precision=lax.Precision.HIGHEST)
        convolved = convolved + jnp.einsum(
            "tng,ngk->tgk", carry_coef, modal_state, precision=lax.Precision.HIGHEST
        )
        new_state = block_decay[:, :, None] * modal_state + jnp.einsum(
            "tng,tgk->ngk", feed_coef, grouped[fir_len:], precision=lax.Precision.HIGHEST
        )
        result = (inputs_f + features[:, 0] * convolved.reshape(block_len, local)).astype(
            jnp.bfloat16
        )
        proj_cache = jnp.where(is_live, extended[block_len:], proj_cache)
        kv_cache = jnp.where(is_live, window[block_len:], kv_cache)
        modal_state = jnp.where(is_live, new_state, modal_state)
        out_buffer = jnp.where(
            is_live, lax.dynamic_update_slice_in_dim(out_buffer, result, begin_row, 0), out_buffer
        )
        passed = shifted(result, "section", 1)
        return ((passed, proj_cache, kv_cache, modal_state, out_buffer), None)

    initial = (
        jnp.zeros((block_len, local), jnp.bfloat16),
        jnp.zeros((2, 3, local), jnp.float32),
        jnp.zeros((fir_len, local), jnp.float32),
        jnp.zeros((residues.shape[1], groups_local, group_size), jnp.float32),
        jnp.zeros((block_len * num_blocks, local), jnp.bfloat16),
    )
    finals, unused = lax.scan(turn, initial, jnp.arange(num_blocks + sections - 1, dtype=jnp.int32))
    return finals[4][None]


def solution(mesh):
    return jax.shard_map(
        body,
        mesh=mesh,
        in_specs=(
            P(None, "chan"),
            P("section", "chan"),
            P("section", None, None, "chan"),
            P("section", None, None, "chan"),
            P("section", None, "chan"),
            P("section", None, "chan"),
            P("section", None, "chan"),
        ),
        out_specs=P("section", None, "chan"),
        check_vma=False,
    )
```

profile of v0, /device:TPU:1, one launch (start us, length us, event | category | flops | bytes accessed | tf_op | source)
XLA Modules:
  0.0 1730.6 jit_solution(16256413265977966794)
XLA Ops:
  7.2 16.7 copy.26
  41.1 41.1 %gather_fusion.1 = f32[12288,16]{1,0:T(8,128)} fusion(f32[16,64]{0,1:T(8,128)S(1)} %multiply_reduce_fusion, s32[12288]{0:T(1024)S(1)} %broadcast_clamp_fusion), kind=kCustom, calls=%fused_computation.1 | custom fusion | bytes 1622016 | tf_op jit(solution)/shard_map/gather | solution.py:43
  87.5 41.1 %gather_fusion = f32[12288,16]{1,0:T(8,128)} fusion(f32[16,128]{0,1:T(8,128)S(1)} %bitcast.82, s32[12288]{0:T(1024)S(1)} %broadcast_clamp_fusion.1), kind=kCustom, calls=%fused_computation | custom fusion | bytes 1622016 | tf_op jit(solution)/shard_map/gather | solution.py:37
  133.9 1589.2 %while.22 = (s32[]{:T(128)}, bf16[64,256]{1,0:T(8,128)(2,1)S(1)}, f32[2,3,256]{2,1,0:T(4,128)S(1)}, f32[128,256]{0,1:T(8,128)S(1)}, f32[16,16,16]{0,2,1:T(8,128)...) while((s32[]{:T(128)}, bf16[64,256]{1,0:T(8,128)(2,1)S(1)}, ...), condition=%wide.region_3.4_spmd.clone.clone.clone, body=%wide.region_0.3_spmd.clone.clone.clone.sunk | while | flops 850173312 | bytes 21374916 | solution.py:103
  136.1 64.3 %psum.12 = f32[64]{0:T(128)S(1)} all-reduce(f32[64]{0:T(128)S(1)} %get-tuple-element.554), channel_id=1, replica_groups=mesh['section'=8,'chan'=32] {'chan'}, use_global_device_ids=true, to_apply=%region_2.2 | all-reduce | flops 64 | bytes 512 | tf_op jit(solution)/shard_map/while/body/eval_jaxpr/psum | solution.py:64
  201.2 76.1 %all-gather.2.cloned.1.call-done = bf16[64,8192]{1,0:T(8,128)(2,1)} async-done(((bf16[64,256]{1,0:T(8,128)(2,1)}), bf16[64,8192]{1,0:T(8,128)(2,1)}) %all-gather.2.cloned.1.call-update) | async-done | bytes 1048592 | tf_op jit(solution)/shard_map/while/body/eval_jaxpr/all_gather | solution.py:68
  297.3 59.9 %psum.12 = f32[64]{0:T(128)S(1)} all-reduce(f32[64]{0:T(128)S(1)} %get-tuple-element.554), channel_id=1, replica_groups=mesh['section'=8,'chan'=32] {'chan'}, use_global_device_ids=true, to_apply=%region_2.2 | all-reduce | flops 64 | bytes 512 | tf_op jit(solution)/shard_map/while/body/eval_jaxpr/psum | solution.py:64
  357.9 78.0 %all-gather.2.cloned.1.call-done = bf16[64,8192]{1,0:T(8,128)(2,1)} async-done(((bf16[64,256]{1,0:T(8,128)(2,1)}), bf16[64,8192]{1,0:T(8,128)(2,1)}) %all-gather.2.cloned.1.call-update) | async-done | bytes 1048592 | tf_op jit(solution)/shard_map/while/body/eval_jaxpr/all_gather | solution.py:68
  455.9 59.9 %psum.12 = f32[64]{0:T(128)S(1)} all-reduce(f32[64]{0:T(128)S(1)} %get-tuple-element.554), channel_id=1, replica_groups=mesh['section'=8,'chan'=32] {'chan'}, use_global_device_ids=true, to_apply=%region_2.2 | all-reduce | flops 64 | bytes 512 | tf_op jit(solution)/shard_map/while/body/eval_jaxpr/psum | solution.py:64
  516.6 78.0 %all-gather.2.cloned.1.call-done = bf16[64,8192]{1,0:T(8,128)(2,1)} async-done(((bf16[64,256]{1,0:T(8,128)(2,1)}), bf16[64,8192]{1,0:T(8,128)(2,1)}) %all-gather.2.cloned.1.call-update) | async-done | bytes 1048592 | tf_op jit(solution)/shard_map/while/body/eval_jaxpr/all_gather | solution.py:68
  614.6 59.9 %psum.12 = f32[64]{0:T(128)S(1)} all-reduce(f32[64]{0:T(128)S(1)} %get-tuple-element.554), channel_id=1, replica_groups=mesh['section'=8,'chan'=32] {'chan'}, use_global_device_ids=true, to_apply=%region_2.2 | all-reduce | flops 64 | bytes 512 | tf_op jit(solution)/shard_map/while/body/eval_jaxpr/psum | solution.py:64
  675.2 78.0 %all-gather.2.cloned.1.call-done = bf16[64,8192]{1,0:T(8,128)(2,1)} async-done(((bf16[64,256]{1,0:T(8,128)(2,1)}), bf16[64,8192]{1,0:T(8,128)(2,1)}) %all-gather.2.cloned.1.call-update) | async-done | bytes 1048592 | tf_op jit(solution)/shard_map/while/body/eval_jaxpr/all_gather | solution.py:68
  773.3 59.9 %psum.12 = f32[64]{0:T(128)S(1)} all-reduce(f32[64]{0:T(128)S(1)} %get-tuple-element.554), channel_id=1, replica_groups=mesh['section'=8,'chan'=32] {'chan'}, use_global_device_ids=true, to_apply=%region_2.2 | all-reduce | flops 64 | bytes 512 | tf_op jit(solution)/shard_map/while/body/eval_jaxpr/psum | solution.py:64
  833.9 78.0 %all-gather.2.cloned.1.call-done = bf16[64,8192]{1,0:T(8,128)(2,1)} async-done(((bf16[64,256]{1,0:T(8,128)(2,1)}), bf16[64,8192]{1,0:T(8,128)(2,1)}) %all-gather.2.cloned.1.call-update) | async-done | bytes 1048592 | tf_op jit(solution)/shard_map/while/body/eval_jaxpr/all_gather | solution.py:68
  931.9 59.9 %psum.12 = f32[64]{0:T(128)S(1)} all-reduce(f32[64]{0:T(128)S(1)} %get-tuple-element.554), channel_id=1, replica_groups=mesh['section'=8,'chan'=32] {'chan'}, use_global_device_ids=true, to_apply=%region_2.2 | all-reduce | flops 64 | bytes 512 | tf_op jit(solution)/shard_map/while/body/eval_jaxpr/psum | solution.py:64
  992.6 78.0 %all-gather.2.cloned.1.call-done = bf16[64,8192]{1,0:T(8,128)(2,1)} async-done(((bf16[64,256]{1,0:T(8,128)(2,1)}), bf16[64,8192]{1,0:T(8,128)(2,1)}) %all-gather.2.cloned.1.call-update) | async-done | bytes 1048592 | tf_op jit(solution)/shard_map/while/body/eval_jaxpr/all_gather | solution.py:68
  1090.6 59.9 %psum.12 = f32[64]{0:T(128)S(1)} all-reduce(f32[64]{0:T(128)S(1)} %get-tuple-element.554), channel_id=1, replica_groups=mesh['section'=8,'chan'=32] {'chan'}, use_global_device_ids=true, to_apply=%region_2.2 | all-reduce | flops 64 | bytes 512 | tf_op jit(solution)/shard_map/while/body/eval_jaxpr/psum | solution.py:64
  1151.2 78.0 %all-gather.2.cloned.1.call-done = bf16[64,8192]{1,0:T(8,128)(2,1)} async-done(((bf16[64,256]{1,0:T(8,128)(2,1)}), bf16[64,8192]{1,0:T(8,128)(2,1)}) %all-gather.2.cloned.1.call-update) | async-done | bytes 1048592 | tf_op jit(solution)/shard_map/while/body/eval_jaxpr/all_gather | solution.py:68
  1249.3 59.9 %psum.12 = f32[64]{0:T(128)S(1)} all-reduce(f32[64]{0:T(128)S(1)} %get-tuple-element.554), channel_id=1, replica_groups=mesh['section'=8,'chan'=32] {'chan'}, use_global_device_ids=true, to_apply=%region_2.2 | all-reduce | flops 64 | bytes 512 | tf_op jit(solution)/shard_map/while/body/eval_jaxpr/psum | solution.py:64
  1309.9 78.0 %all-gather.2.cloned.1.call-done = bf16[64,8192]{1,0:T(8,128)(2,1)} async-done(((bf16[64,256]{1,0:T(8,128)(2,1)}), bf16[64,8192]{1,0:T(8,128)(2,1)}) %all-gather.2.cloned.1.call-update) | async-done | bytes 1048592 | tf_op jit(solution)/shard_map/while/body/eval_jaxpr/all_gather | solution.py:68
  1407.9 59.9 %psum.12 = f32[64]{0:T(128)S(1)} all-reduce(f32[64]{0:T(128)S(1)} %get-tuple-element.554), channel_id=1, replica_groups=mesh['section'=8,'chan'=32] {'chan'}, use_global_device_ids=true, to_apply=%region_2.2 | all-reduce | flops 64 | bytes 512 | tf_op jit(solution)/shard_map/while/body/eval_jaxpr/psum | solution.py:64
  1468.6 78.0 %all-gather.2.cloned.1.call-done = bf16[64,8192]{1,0:T(8,128)(2,1)} async-done(((bf16[64,256]{1,0:T(8,128)(2,1)}), bf16[64,8192]{1,0:T(8,128)(2,1)}) %all-gather.2.cloned.1.call-update) | async-done | bytes 1048592 | tf_op jit(solution)/shard_map/while/body/eval_jaxpr/all_gather | solution.py:68
  1566.6 59.9 %psum.12 = f32[64]{0:T(128)S(1)} all-reduce(f32[64]{0:T(128)S(1)} %get-tuple-element.554), channel_id=1, replica_groups=mesh['section'=8,'chan'=32] {'chan'}, use_global_device_ids=true, to_apply=%region_2.2 | all-reduce | flops 64 | bytes 512 | tf_op jit(solution)/shard_map/while/body/eval_jaxpr/psum | solution.py:64
  1627.2 78.0 %all-gather.2.cloned.1.call-done = bf16[64,8192]{1,0:T(8,128)(2,1)} async-done(((bf16[64,256]{1,0:T(8,128)(2,1)}), bf16[64,8192]{1,0:T(8,128)(2,1)}) %all-gather.2.cloned.1.call-update) | async-done | bytes 1048592 | tf_op jit(solution)/shard_map/while/body/eval_jaxpr/all_gather | solution.py:68
  (299 shorter events, 228.8 us)
Async XLA Ops:
  23.9 16.7 copy-start.4
  23.9 16.8 copy-start.1
  40.6 46.6 %copy-start.3 = (f32[1,128,16]{1,2,0:T(8,128)S(1)}, f32[1,128,16]{1,2,0:T(8,128)}, u32[]{:S(2)}) copy-start(f32[1,128,16]{1,2,0:T(8,128)} %param.13) | copy-start | bytes 24580
  82.3 51.6 %copy-start.2 = (bf16[1,256]{1,0:T(2,128)(2,1)S(1)}, bf16[1,256]{1,0:T(2,128)(2,1)}, u32[]{:S(2)}) copy-start(bf16[1,256]{1,0:T(2,128)(2,1)} %param.10) | copy-start | bytes 1540
  133.9 143.3 %all-gather.2.cloned.1.call-start = ((), (), s32[]{:S(2)}) async-start(), calls=%async_computation | async-start | bytes 1081344 | tf_op jit(solution)/shard_map/while/body/eval_jaxpr/all_gather | solution.py:68
  286.4 8.7 collective-permute-start
  295.1 140.8 %all-gather.2.cloned.1.call-start = ((), (), s32[]{:S(2)}) async-start(), calls=%async_computation | async-start | bytes 1081344 | tf_op jit(solution)/shard_map/while/body/eval_jaxpr/all_gather | solution.py:68
  445.0 8.7 collective-permute-start
  453.8 140.8 %all-gather.2.cloned.1.call-start = ((), (), s32[]{:S(2)}) async-start(), calls=%async_computation | async-start | bytes 1081344 | tf_op jit(solution)/shard_map/while/body/eval_jaxpr/all_gather | solution.py:68
  603.7 8.7 collective-permute-start
  612.5 140.8 %all-gather.2.cloned.1.call-start = ((), (), s32[]{:S(2)}) async-start(), calls=%async_computation | async-start | bytes 1081344 | tf_op jit(solution)/shard_map/while/body/eval_jaxpr/all_gather | solution.py:68
  762.4 8.7 collective-permute-start
  771.1 140.8 %all-gather.2.cloned.1.call-start = ((), (), s32[]{:S(2)}) async-start(), calls=%async_computation | async-start | bytes 1081344 | tf_op jit(solution)/shard_map/while/body/eval_jaxpr/all_gather | solution.py:68
  921.0 8.7 collective-permute-start
  929.8 140.8 %all-gather.2.cloned.1.call-start = ((), (), s32[]{:S(2)}) async-start(), calls=%async_computation | async-start | bytes 1081344 | tf_op jit(solution)/shard_map/while/body/eval_jaxpr/all_gather | solution.py:68
  1079.7 8.7 collective-permute-start
  1088.5 140.8 %all-gather.2.cloned.1.call-start = ((), (), s32[]{:S(2)}) async-start(), calls=%async_computation | async-start | bytes 1081344 | tf_op jit(solution)/shard_map/while/body/eval_jaxpr/all_gather | solution.py:68
  1238.4 8.7 collective-permute-start
  1247.1 140.8 %all-gather.2.cloned.1.call-start = ((), (), s32[]{:S(2)}) async-start(), calls=%async_computation | async-start | bytes 1081344 | tf_op jit(solution)/shard_map/while/body/eval_jaxpr/all_gather | solution.py:68
  1397.0 8.7 collective-permute-start
  1405.8 140.8 %all-gather.2.cloned.1.call-start = ((), (), s32[]{:S(2)}) async-start(), calls=%async_computation | async-start | bytes 1081344 | tf_op jit(solution)/shard_map/while/body/eval_jaxpr/all_gather | solution.py:68
  1555.7 8.7 collective-permute-start
  1564.4 140.8 %all-gather.2.cloned.1.call-start = ((), (), s32[]{:S(2)}) async-start(), calls=%async_computation | async-start | bytes 1081344 | tf_op jit(solution)/shard_map/while/body/eval_jaxpr/all_gather | solution.py:68
  1714.4 8.7 collective-permute-start
  (1 other events, 0.6 us)
Sparse Core Ops, SparseCore 0:
  201.3 75.9 all-gather.1
  358.0 77.8 all-gather.1
  516.6 77.8 all-gather.1
  675.3 77.8 all-gather.1
  834.0 77.8 all-gather.1
  992.6 77.8 all-gather.1
  1151.3 77.8 all-gather.1
  1310.0 77.8 all-gather.1
  1468.6 77.8 all-gather.1
  1627.3 77.8 all-gather.1
where the time goes:
time: 1730 us
  waiting for transfers between devices  783 us (45%)
  blocking collectives  603 us (35%)
  local copies, waits for them, and re-layouts  136 us (8%)
  matrix products  88.7 us (5%)
  starting transfers between devices  77.4 us (4%)
  other arithmetic  20.9 us (1%)
    all_gather x10, waiting for transfers between devices, turn(): projected = add_rows(lax.all_gather(normed, 'chan', axis=1, tiled=True))  778 us
    psum x10, blocking collectives, turn(): squares = lax.psum(partial_sq, 'chan')  603 us
    ppermute x10, starting transfers between devices, shifted(): lax.ppermute(value, axis, [(source, source + steps) for source in range(i...  77.3 us
    dot_general x10, matrix products, add_rows(): return jnp.dot(shard_piece, weight, preferred_element_type=jnp.float32)  71.6 us
    gather x2, local copies, waits for them, and re-layouts, body(): modal.T[:, jnp.clip(inner_lag, 0, block_len - 1)]  46 us
    gather x2, local copies, waits for them, and re-layouts, body(): fir_section.T[:, jnp.clip(fir_lag, 0, fir_len - 1)]  46 us
    unnamed x16, local copies, waits for them, and re-layouts  34.9 us
  transfers between devices with their start and end apart: 20, of which 20 were waited for; matrix products, arithmetic and copies ran while one was open for 0% of the time, Pallas kernels for 0%

commit v1 on v0

--- a/solution.py
+++ b/solution.py
@@ -65,7 +65,11 @@
         normed = (
             inputs_f * lax.rsqrt(squares[:, None] / width + EPSILON) * norm_gain.astype(jnp.float32)
         ).astype(jnp.bfloat16)
-        projected = add_rows(lax.all_gather(normed, "chan", axis=1, tiled=True))
+        projected = add_rows(
+            jnp.concatenate(
+                lax.all_to_all(jnp.stack([normed] * lax.axis_size("chan")), "chan", 0, 0), axis=1
+            )
+        )
         projected = projected.reshape(block_len, 3, local)
         extended = jnp.concatenate([proj_cache, projected], axis=0)
         features = (

time: 1730 us -> 1270 us (0.73)
  waiting for transfers between devices: 783 us -> 199 us
  starting transfers between devices: 77.4 us -> 230 us
  blocking collectives: 603 us -> 579 us
    all_gather x10 -> x0, waiting for transfers between devices: 778 us -> none  [turn(): projected = add_rows(lax.all_gather(normed, 'chan', axis=1, tiled=True))]
    all_to_all x0 -> x10, waiting for transfers between devices: none -> 195 us  [turn(): lax.all_to_all(jnp.stack([normed] * lax.axis_size('chan')), 'chan', 0, 0)]
    ppermute x10, starting transfers between devices: 77.3 us -> 177 us  [shifted(): lax.ppermute(value, axis, [(source, source + steps) for source in range(i...]
    all_to_all x0 -> x10, starting transfers between devices: none -> 53 us  [turn(): lax.all_to_all(jnp.stack([normed] * lax.axis_size('chan')), 'chan', 0, 0)]
    psum x10, blocking collectives: 603 us -> 579 us  [turn(): squares = lax.psum(partial_sq, 'chan')]
where the time goes in v1:
time: 1270 us; the launch traced here: 1260 us
  blocking collectives  579 us (46%)
  starting transfers between devices  230 us (18%)
  waiting for transfers between devices  199 us (16%)
  local copies, waits for them, and re-layouts  148 us (12%)
  matrix products  85.5 us (7%)
  other arithmetic  14.7 us (1%)
    psum x10, blocking collectives, turn(): squares = lax.psum(partial_sq, 'chan')  579 us
    all_to_all x10, waiting for transfers between devices, turn(): lax.all_to_all(jnp.stack([normed] * lax.axis_size('chan')), 'chan', 0, 0)  195 us
    ppermute x10, starting transfers between devices, shifted(): lax.ppermute(value, axis, [(source, source + steps) for source in range(i...  177 us
    dot_general x10, matrix products, add_rows(): return jnp.dot(shard_piece, weight, preferred_element_type=jnp.float32)  68.4 us
    all_to_all x10, starting transfers between devices, turn(): lax.all_to_all(jnp.stack([normed] * lax.axis_size('chan')), 'chan', 0, 0)  53 us
    gather x2, local copies, waits for them, and re-layouts, body(): modal.T[:, jnp.clip(inner_lag, 0, block_len - 1)]  46.2 us
    gather x2, local copies, waits for them, and re-layouts, body(): fir_section.T[:, jnp.clip(fir_lag, 0, fir_len - 1)]  46.2 us
    unnamed x16, local copies, waits for them, and re-layouts  35 us
  transfers between devices with their start and end apart: 20, of which 20 were waited for; matrix products, arithmetic and copies ran while one was open for 0% of the time, Pallas kernels for 0%

profile of v1, /device:TPU:1, one launch (start us, length us, event | category | flops | bytes accessed | tf_op | source)
XLA Modules:
  0.0 1264.2 jit_solution(18432028588006488724)
XLA Ops:
  34.6 41.3 %gather_fusion.1 = f32[12288,16]{1,0:T(8,128)} fusion(f32[16,64]{0,1:T(8,128)S(1)} %multiply_reduce_fusion, s32[12288]{0:T(1024)S(1)} %broadcast_clamp_fusion), kind=kCustom, calls=%fused_computation.1 | custom fusion | bytes 1622016 | tf_op jit(solution)/shard_map/gather | solution.py:43
  81.2 41.3 %gather_fusion = f32[12288,16]{1,0:T(8,128)} fusion(f32[16,128]{0,1:T(8,128)S(1)} %bitcast.89, s32[12288]{0:T(1024)S(1)} %broadcast_clamp_fusion.1), kind=kCustom, calls=%fused_computation | custom fusion | bytes 1622016 | tf_op jit(solution)/shard_map/gather | solution.py:37
  127.8 1135.8 %while.22 = (s32[]{:T(128)}, bf16[64,256]{1,0:T(8,128)(2,1)S(1)}, f32[2,3,256]{2,1,0:T(4,128)S(1)}, f32[128,256]{0,1:T(8,128)S(1)}, f32[16,16,16]{0,2,1:T(8,128)...) while((s32[]{:T(128)}, bf16[64,256]{1,0:T(8,128)(2,1)S(1)}, ...), condition=%wide.region_3.4_spmd.clone.clone.clone, body=%wide.region_0.3_spmd.clone.clone.clone.sunk | while | flops 850173312 | bytes 24455100 | solution.py:107
  129.8 64.3 %psum.12 = f32[64]{0:T(128)S(1)} all-reduce(f32[64]{0:T(128)S(1)} %get-tuple-element.574), channel_id=1, replica_groups=mesh['section'=8,'chan'=32] {'chan'}, use_global_device_ids=true, to_apply=%region_2.2 | all-reduce | flops 64 | bytes 512 | tf_op jit(solution)/shard_map/while/body/eval_jaxpr/psum | solution.py:64
  225.6 19.4 %collective-permute-start = (bf16[64,256]{1,0:T(8,128)(2,1)S(1)}, bf16[64,256]{1,0:T(8,128)(2,1)S(1)}, u32[]{:S(2)}, u32[]{:S(2)}) collective-permute-start(bf16[64,256]{1,0:T(8,128)(2,1)S(1)} %get-tuple-element.581), channel_id=1, source_target_pairs={{0,32},{32,64},{64,96},{96,128},{128,160},{160,192},{192,224},{1,3... | collective-permute-start | bytes 98312 | tf_op jit(solution)/shard_map/while/body/eval_jaxpr/ppermute | solution.py:14
  248.0 57.2 %psum.12 = f32[64]{0:T(128)S(1)} all-reduce(f32[64]{0:T(128)S(1)} %get-tuple-element.574), channel_id=1, replica_groups=mesh['section'=8,'chan'=32] {'chan'}, use_global_device_ids=true, to_apply=%region_2.2 | all-reduce | flops 64 | bytes 512 | tf_op jit(solution)/shard_map/while/body/eval_jaxpr/psum | solution.py:64
  337.8 20.1 %collective-permute-start = (bf16[64,256]{1,0:T(8,128)(2,1)S(1)}, bf16[64,256]{1,0:T(8,128)(2,1)S(1)}, u32[]{:S(2)}, u32[]{:S(2)}) collective-permute-start(bf16[64,256]{1,0:T(8,128)(2,1)S(1)} %get-tuple-element.581), channel_id=1, source_target_pairs={{0,32},{32,64},{64,96},{96,128},{128,160},{160,192},{192,224},{1,3... | collective-permute-start | bytes 98312 | tf_op jit(solution)/shard_map/while/body/eval_jaxpr/ppermute | solution.py:14
  360.9 57.2 %psum.12 = f32[64]{0:T(128)S(1)} all-reduce(f32[64]{0:T(128)S(1)} %get-tuple-element.574), channel_id=1, replica_groups=mesh['section'=8,'chan'=32] {'chan'}, use_global_device_ids=true, to_apply=%region_2.2 | all-reduce | flops 64 | bytes 512 | tf_op jit(solution)/shard_map/while/body/eval_jaxpr/psum | solution.py:64
  425.2 18.5 %all-to-all-done = bf16[32,64,256]{2,1,0:T(8,128)(2,1)S(1)} async-done(((bf16[32,64,256]{2,1,0:T(8,128)(2,1)}), bf16[32,64,256]{2,1,0:T(8,128)(2,1)S(1)}, u32[]{:S(2)}, u32[]{:S(2)}) %all-to-all-start) | async-done | bytes 1048608 | tf_op jit(solution)/shard_map/while/body/eval_jaxpr/all_to_all | solution.py:70
  452.6 18.1 %collective-permute-start = (bf16[64,256]{1,0:T(8,128)(2,1)S(1)}, bf16[64,256]{1,0:T(8,128)(2,1)S(1)}, u32[]{:S(2)}, u32[]{:S(2)}) collective-permute-start(bf16[64,256]{1,0:T(8,128)(2,1)S(1)} %get-tuple-element.581), channel_id=1, source_target_pairs={{0,32},{32,64},{64,96},{96,128},{128,160},{160,192},{192,224},{1,3... | collective-permute-start | bytes 98312 | tf_op jit(solution)/shard_map/while/body/eval_jaxpr/ppermute | solution.py:14
  473.7 57.1 %psum.12 = f32[64]{0:T(128)S(1)} all-reduce(f32[64]{0:T(128)S(1)} %get-tuple-element.574), channel_id=1, replica_groups=mesh['section'=8,'chan'=32] {'chan'}, use_global_device_ids=true, to_apply=%region_2.2 | all-reduce | flops 64 | bytes 512 | tf_op jit(solution)/shard_map/while/body/eval_jaxpr/psum | solution.py:64
  538.0 19.7 %all-to-all-done = bf16[32,64,256]{2,1,0:T(8,128)(2,1)S(1)} async-done(((bf16[32,64,256]{2,1,0:T(8,128)(2,1)}), bf16[32,64,256]{2,1,0:T(8,128)(2,1)S(1)}, u32[]{:S(2)}, u32[]{:S(2)}) %all-to-all-start) | async-done | bytes 1048608 | tf_op jit(solution)/shard_map/while/body/eval_jaxpr/all_to_all | solution.py:70
  587.1 57.1 %psum.12 = f32[64]{0:T(128)S(1)} all-reduce(f32[64]{0:T(128)S(1)} %get-tuple-element.574), channel_id=1, replica_groups=mesh['section'=8,'chan'=32] {'chan'}, use_global_device_ids=true, to_apply=%region_2.2 | all-reduce | flops 64 | bytes 512 | tf_op jit(solution)/shard_map/while/body/eval_jaxpr/psum | solution.py:64
  651.5 20.9 %all-to-all-done = bf16[32,64,256]{2,1,0:T(8,128)(2,1)S(1)} async-done(((bf16[32,64,256]{2,1,0:T(8,128)(2,1)}), bf16[32,64,256]{2,1,0:T(8,128)(2,1)S(1)}, u32[]{:S(2)}, u32[]{:S(2)}) %all-to-all-start) | async-done | bytes 1048608 | tf_op jit(solution)/shard_map/while/body/eval_jaxpr/all_to_all | solution.py:70
  700.5 57.1 %psum.12 = f32[64]{0:T(128)S(1)} all-reduce(f32[64]{0:T(128)S(1)} %get-tuple-element.574), channel_id=1, replica_groups=mesh['section'=8,'chan'=32] {'chan'}, use_global_device_ids=true, to_apply=%region_2.2 | all-reduce | flops 64 | bytes 512 | tf_op jit(solution)/shard_map/while/body/eval_jaxpr/psum | solution.py:64
  764.3 20.0 %all-to-all-done = bf16[32,64,256]{2,1,0:T(8,128)(2,1)S(1)} async-done(((bf16[32,64,256]{2,1,0:T(8,128)(2,1)}), bf16[32,64,256]{2,1,0:T(8,128)(2,1)S(1)}, u32[]{:S(2)}, u32[]{:S(2)}) %all-to-all-start) | async-done | bytes 1048608 | tf_op jit(solution)/shard_map/while/body/eval_jaxpr/all_to_all | solution.py:70
  813.3 57.2 %psum.12 = f32[64]{0:T(128)S(1)} all-reduce(f32[64]{0:T(128)S(1)} %get-tuple-element.574), channel_id=1, replica_groups=mesh['section'=8,'chan'=32] {'chan'}, use_global_device_ids=true, to_apply=%region_2.2 | all-reduce | flops 64 | bytes 512 | tf_op jit(solution)/shard_map/while/body/eval_jaxpr/psum | solution.py:64
  877.1 20.3 %all-to-all-done = bf16[32,64,256]{2,1,0:T(8,128)(2,1)S(1)} async-done(((bf16[32,64,256]{2,1,0:T(8,128)(2,1)}), bf16[32,64,256]{2,1,0:T(8,128)(2,1)S(1)}, u32[]{:S(2)}, u32[]{:S(2)}) %all-to-all-start) | async-done | bytes 1048608 | tf_op jit(solution)/shard_map/while/body/eval_jaxpr/all_to_all | solution.py:70
  926.1 57.2 %psum.12 = f32[64]{0:T(128)S(1)} all-reduce(f32[64]{0:T(128)S(1)} %get-tuple-element.574), channel_id=1, replica_groups=mesh['section'=8,'chan'=32] {'chan'}, use_global_device_ids=true, to_apply=%region_2.2 | all-reduce | flops 64 | bytes 512 | tf_op jit(solution)/shard_map/while/body/eval_jaxpr/psum | solution.py:64
  989.9 20.3 %all-to-all-done = bf16[32,64,256]{2,1,0:T(8,128)(2,1)S(1)} async-done(((bf16[32,64,256]{2,1,0:T(8,128)(2,1)}), bf16[32,64,256]{2,1,0:T(8,128)(2,1)S(1)}, u32[]{:S(2)}, u32[]{:S(2)}) %all-to-all-start) | async-done | bytes 1048608 | tf_op jit(solution)/shard_map/while/body/eval_jaxpr/all_to_all | solution.py:70
  1039.5 57.5 %psum.12 = f32[64]{0:T(128)S(1)} all-reduce(f32[64]{0:T(128)S(1)} %get-tuple-element.574), channel_id=1, replica_groups=mesh['section'=8,'chan'=32] {'chan'}, use_global_device_ids=true, to_apply=%region_2.2 | all-reduce | flops 64 | bytes 512 | tf_op jit(solution)/shard_map/while/body/eval_jaxpr/psum | solution.py:64
  1103.4 20.9 %all-to-all-done = bf16[32,64,256]{2,1,0:T(8,128)(2,1)S(1)} async-done(((bf16[32,64,256]{2,1,0:T(8,128)(2,1)}), bf16[32,64,256]{2,1,0:T(8,128)(2,1)S(1)}, u32[]{:S(2)}, u32[]{:S(2)}) %all-to-all-start) | async-done | bytes 1048608 | tf_op jit(solution)/shard_map/while/body/eval_jaxpr/all_to_all | solution.py:70
  1152.4 57.2 %psum.12 = f32[64]{0:T(128)S(1)} all-reduce(f32[64]{0:T(128)S(1)} %get-tuple-element.574), channel_id=1, replica_groups=mesh['section'=8,'chan'=32] {'chan'}, use_global_device_ids=true, to_apply=%region_2.2 | all-reduce | flops 64 | bytes 512 | tf_op jit(solution)/shard_map/while/body/eval_jaxpr/psum | solution.py:64
  1216.2 19.8 %all-to-all-done = bf16[32,64,256]{2,1,0:T(8,128)(2,1)S(1)} async-done(((bf16[32,64,256]{2,1,0:T(8,128)(2,1)}), bf16[32,64,256]{2,1,0:T(8,128)(2,1)S(1)}, u32[]{:S(2)}, u32[]{:S(2)}) %all-to-all-start) | async-done | bytes 1048608 | tf_op jit(solution)/shard_map/while/body/eval_jaxpr/all_to_all | solution.py:70
  (309 shorter events, 376.9 us)
Async XLA Ops:
  17.4 16.7 %copy-start.4 = (f32[1,16,16]{2,1,0:T(8,128)S(1)}, f32[1,16,16]{2,1,0:T(8,128)}, u32[]{:S(2)}) copy-start(f32[1,16,16]{2,1,0:T(8,128)} %param.15) | copy-start | bytes 3076
  17.4 16.8 %copy-start.1 = (f32[1,16,16]{2,1,0:T(8,128)S(1)}, f32[1,16,16]{2,1,0:T(8,128)}, u32[]{:S(2)}) copy-start(f32[1,16,16]{2,1,0:T(8,128)} %param.14) | copy-start | bytes 3076
  34.1 46.8 %copy-start.3 = (f32[1,128,16]{1,2,0:T(8,128)S(1)}, f32[1,128,16]{1,2,0:T(8,128)}, u32[]{:S(2)}) copy-start(f32[1,128,16]{1,2,0:T(8,128)} %param.13) | copy-start | bytes 24580
  76.0 51.8 %copy-start.2 = (bf16[1,256]{1,0:T(2,128)(2,1)S(1)}, bf16[1,256]{1,0:T(2,128)(2,1)}, u32[]{:S(2)}) copy-start(bf16[1,256]{1,0:T(2,128)(2,1)} %param.10) | copy-start | bytes 1540
  195.4 21.3 %all-to-all-start = ((bf16[32,64,256]{2,1,0:T(8,128)(2,1)}), bf16[32,64,256]{2,1,0:T(8,128)(2,1)S(1)}, u32[]{:S(2)}, u32[]{:S(2)}) async-start(bf16[32,64,256]{2,1,0:T(8,128)(2,1)} %stack.6), calls=%async_computation | async-start | bytes 2097152 | tf_op jit(solution)/shard_map/while/body/eval_jaxpr/all_to_all | solution.py:70
  225.6 20.4 %collective-permute-start = (bf16[64,256]{1,0:T(8,128)(2,1)S(1)}, bf16[64,256]{1,0:T(8,128)(2,1)S(1)}, u32[]{:S(2)}, u32[]{:S(2)}) collective-permute-start(bf16[64,256]{1,0:T(8,128)(2,1)S(1)} %get-tuple-element.581), channel_id=1, source_target_pairs={{0,32},{32,64},{64,96},{96,128},{128,160},{160,192},{192,224},{1,3... | collective-permute-start | bytes 98312 | tf_op jit(solution)/shard_map/while/body/eval_jaxpr/ppermute | solution.py:14
  306.4 22.5 %all-to-all-start = ((bf16[32,64,256]{2,1,0:T(8,128)(2,1)}), bf16[32,64,256]{2,1,0:T(8,128)(2,1)S(1)}, u32[]{:S(2)}, u32[]{:S(2)}) async-start(bf16[32,64,256]{2,1,0:T(8,128)(2,1)} %stack.6), calls=%async_computation | async-start | bytes 2097152 | tf_op jit(solution)/shard_map/while/body/eval_jaxpr/all_to_all | solution.py:70
  337.8 21.1 %collective-permute-start = (bf16[64,256]{1,0:T(8,128)(2,1)S(1)}, bf16[64,256]{1,0:T(8,128)(2,1)S(1)}, u32[]{:S(2)}, u32[]{:S(2)}) collective-permute-start(bf16[64,256]{1,0:T(8,128)(2,1)S(1)} %get-tuple-element.581), channel_id=1, source_target_pairs={{0,32},{32,64},{64,96},{96,128},{128,160},{160,192},{192,224},{1,3... | collective-permute-start | bytes 98312 | tf_op jit(solution)/shard_map/while/body/eval_jaxpr/ppermute | solution.py:14
  419.4 24.3 %all-to-all-start = ((bf16[32,64,256]{2,1,0:T(8,128)(2,1)}), bf16[32,64,256]{2,1,0:T(8,128)(2,1)S(1)}, u32[]{:S(2)}, u32[]{:S(2)}) async-start(bf16[32,64,256]{2,1,0:T(8,128)(2,1)} %stack.6), calls=%async_computation | async-start | bytes 2097152 | tf_op jit(solution)/shard_map/while/body/eval_jaxpr/all_to_all | solution.py:70
  452.6 19.1 %collective-permute-start = (bf16[64,256]{1,0:T(8,128)(2,1)S(1)}, bf16[64,256]{1,0:T(8,128)(2,1)S(1)}, u32[]{:S(2)}, u32[]{:S(2)}) collective-permute-start(bf16[64,256]{1,0:T(8,128)(2,1)S(1)} %get-tuple-element.581), channel_id=1, source_target_pairs={{0,32},{32,64},{64,96},{96,128},{128,160},{160,192},{192,224},{1,3... | collective-permute-start | bytes 98312 | tf_op jit(solution)/shard_map/while/body/eval_jaxpr/ppermute | solution.py:14
  532.1 25.5 %all-to-all-start = ((bf16[32,64,256]{2,1,0:T(8,128)(2,1)}), bf16[32,64,256]{2,1,0:T(8,128)(2,1)S(1)}, u32[]{:S(2)}, u32[]{:S(2)}) async-start(bf16[32,64,256]{2,1,0:T(8,128)(2,1)} %stack.6), calls=%async_computation | async-start | bytes 2097152 | tf_op jit(solution)/shard_map/while/body/eval_jaxpr/all_to_all | solution.py:70
  566.5 18.6 %collective-permute-start = (bf16[64,256]{1,0:T(8,128)(2,1)S(1)}, bf16[64,256]{1,0:T(8,128)(2,1)S(1)}, u32[]{:S(2)}, u32[]{:S(2)}) collective-permute-start(bf16[64,256]{1,0:T(8,128)(2,1)S(1)} %get-tuple-element.581), channel_id=1, source_target_pairs={{0,32},{32,64},{64,96},{96,128},{128,160},{160,192},{192,224},{1,3... | collective-permute-start | bytes 98312 | tf_op jit(solution)/shard_map/while/body/eval_jaxpr/ppermute | solution.py:14
  645.5 26.9 %all-to-all-start = ((bf16[32,64,256]{2,1,0:T(8,128)(2,1)}), bf16[32,64,256]{2,1,0:T(8,128)(2,1)S(1)}, u32[]{:S(2)}, u32[]{:S(2)}) async-start(bf16[32,64,256]{2,1,0:T(8,128)(2,1)} %stack.6), calls=%async_computation | async-start | bytes 2097152 | tf_op jit(solution)/shard_map/while/body/eval_jaxpr/all_to_all | solution.py:70
  681.3 17.2 %collective-permute-start = (bf16[64,256]{1,0:T(8,128)(2,1)S(1)}, bf16[64,256]{1,0:T(8,128)(2,1)S(1)}, u32[]{:S(2)}, u32[]{:S(2)}) collective-permute-start(bf16[64,256]{1,0:T(8,128)(2,1)S(1)} %get-tuple-element.581), channel_id=1, source_target_pairs={{0,32},{32,64},{64,96},{96,128},{128,160},{160,192},{192,224},{1,3... | collective-permute-start | bytes 98312 | tf_op jit(solution)/shard_map/while/body/eval_jaxpr/ppermute | solution.py:14
  758.9 25.4 %all-to-all-start = ((bf16[32,64,256]{2,1,0:T(8,128)(2,1)}), bf16[32,64,256]{2,1,0:T(8,128)(2,1)S(1)}, u32[]{:S(2)}, u32[]{:S(2)}) async-start(bf16[32,64,256]{2,1,0:T(8,128)(2,1)} %stack.6), calls=%async_computation | async-start | bytes 2097152 | tf_op jit(solution)/shard_map/while/body/eval_jaxpr/all_to_all | solution.py:70
  793.1 18.1 %collective-permute-start = (bf16[64,256]{1,0:T(8,128)(2,1)S(1)}, bf16[64,256]{1,0:T(8,128)(2,1)S(1)}, u32[]{:S(2)}, u32[]{:S(2)}) collective-permute-start(bf16[64,256]{1,0:T(8,128)(2,1)S(1)} %get-tuple-element.581), channel_id=1, source_target_pairs={{0,32},{32,64},{64,96},{96,128},{128,160},{160,192},{192,224},{1,3... | collective-permute-start | bytes 98312 | tf_op jit(solution)/shard_map/while/body/eval_jaxpr/ppermute | solution.py:14
  871.8 25.6 %all-to-all-start = ((bf16[32,64,256]{2,1,0:T(8,128)(2,1)}), bf16[32,64,256]{2,1,0:T(8,128)(2,1)S(1)}, u32[]{:S(2)}, u32[]{:S(2)}) async-start(bf16[32,64,256]{2,1,0:T(8,128)(2,1)} %stack.6), calls=%async_computation | async-start | bytes 2097152 | tf_op jit(solution)/shard_map/while/body/eval_jaxpr/all_to_all | solution.py:70
  906.3 17.8 %collective-permute-start = (bf16[64,256]{1,0:T(8,128)(2,1)S(1)}, bf16[64,256]{1,0:T(8,128)(2,1)S(1)}, u32[]{:S(2)}, u32[]{:S(2)}) collective-permute-start(bf16[64,256]{1,0:T(8,128)(2,1)S(1)} %get-tuple-element.581), channel_id=1, source_target_pairs={{0,32},{32,64},{64,96},{96,128},{128,160},{160,192},{192,224},{1,3... | collective-permute-start | bytes 98312 | tf_op jit(solution)/shard_map/while/body/eval_jaxpr/ppermute | solution.py:14
  984.6 25.7 %all-to-all-start = ((bf16[32,64,256]{2,1,0:T(8,128)(2,1)}), bf16[32,64,256]{2,1,0:T(8,128)(2,1)S(1)}, u32[]{:S(2)}, u32[]{:S(2)}) async-start(bf16[32,64,256]{2,1,0:T(8,128)(2,1)} %stack.6), calls=%async_computation | async-start | bytes 2097152 | tf_op jit(solution)/shard_map/while/body/eval_jaxpr/all_to_all | solution.py:70
  1019.1 18.4 %collective-permute-start = (bf16[64,256]{1,0:T(8,128)(2,1)S(1)}, bf16[64,256]{1,0:T(8,128)(2,1)S(1)}, u32[]{:S(2)}, u32[]{:S(2)}) collective-permute-start(bf16[64,256]{1,0:T(8,128)(2,1)S(1)} %get-tuple-element.581), channel_id=1, source_target_pairs={{0,32},{32,64},{64,96},{96,128},{128,160},{160,192},{192,224},{1,3... | collective-permute-start | bytes 98312 | tf_op jit(solution)/shard_map/while/body/eval_jaxpr/ppermute | solution.py:14
  1098.3 26.0 %all-to-all-start = ((bf16[32,64,256]{2,1,0:T(8,128)(2,1)}), bf16[32,64,256]{2,1,0:T(8,128)(2,1)S(1)}, u32[]{:S(2)}, u32[]{:S(2)}) async-start(bf16[32,64,256]{2,1,0:T(8,128)(2,1)} %stack.6), calls=%async_computation | async-start | bytes 2097152 | tf_op jit(solution)/shard_map/while/body/eval_jaxpr/all_to_all | solution.py:70
  1133.1 17.2 %collective-permute-start = (bf16[64,256]{1,0:T(8,128)(2,1)S(1)}, bf16[64,256]{1,0:T(8,128)(2,1)S(1)}, u32[]{:S(2)}, u32[]{:S(2)}) collective-permute-start(bf16[64,256]{1,0:T(8,128)(2,1)S(1)} %get-tuple-element.581), channel_id=1, source_target_pairs={{0,32},{32,64},{64,96},{96,128},{128,160},{160,192},{192,224},{1,3... | collective-permute-start | bytes 98312 | tf_op jit(solution)/shard_map/while/body/eval_jaxpr/ppermute | solution.py:14
  1210.8 25.1 %all-to-all-start = ((bf16[32,64,256]{2,1,0:T(8,128)(2,1)}), bf16[32,64,256]{2,1,0:T(8,128)(2,1)S(1)}, u32[]{:S(2)}, u32[]{:S(2)}) async-start(bf16[32,64,256]{2,1,0:T(8,128)(2,1)} %stack.6), calls=%async_computation | async-start | bytes 2097152 | tf_op jit(solution)/shard_map/while/body/eval_jaxpr/all_to_all | solution.py:70
  1244.8 18.8 %collective-permute-start = (bf16[64,256]{1,0:T(8,128)(2,1)S(1)}, bf16[64,256]{1,0:T(8,128)(2,1)S(1)}, u32[]{:S(2)}, u32[]{:S(2)}) collective-permute-start(bf16[64,256]{1,0:T(8,128)(2,1)S(1)} %get-tuple-element.581), channel_id=1, source_target_pairs={{0,32},{32,64},{64,96},{96,128},{128,160},{160,192},{192,224},{1,3... | collective-permute-start | bytes 98312 | tf_op jit(solution)/shard_map/while/body/eval_jaxpr/ppermute | solution.py:14
  (1 other events, 0.6 us)
